TPU v7x, 1024 devices: a whole 4x8x16 slice. The times are simulated.
1024 devices in a mesh: dp: 32 (over y, z_hi, core), cuts: 32 (over z_lo, x).
Axes of the slice: x: 4, y: 8, z: 16 (z_hi: 2, z_lo: 8; z = z_hi * 8 + z_lo), core: 2. Of those that a mesh axis runs over, the one named last changes fastest.
Arguments:
- hidden: bfloat16 [32, 256, 8192], P('dp', None, 'cuts'), may hold values from -6 to 6
- down_weight: bfloat16 [32, 8192, 3072], P('dp', 'cuts'), may hold values from -0.0625 to 0.0625
- expert_ids: int32 [4096, 2], P('dp'), may hold values from 0 to 63, all different within a row; in each aligned block of 128 rows (0 to 127, 128 to 255, ...) at most 8 rows name the same one
- combine: float32 [4096, 2], P('dp'), may hold values from 0.1 to 1
- out_grad: bfloat16 [4096, 3072], P('dp', 'cuts'), may hold values from -6 to 6
Outputs:
- mixed: bfloat16 [4096, 3072], P('dp', 'cuts')
- hidden_grad: bfloat16 [32, 256, 8192], P('dp', None, 'cuts')
- weight_grad: bfloat16 [32, 8192, 3072], P('dp', 'cuts')
Inputs may be any that keep to these rules, and one draw needn't show every extreme that they name: `expert_ids`: the two ids of a row differ. Among the 256 pairs of one index of dp, no expert is named more than 8 times, a bound that some block reaches.
All inputs are finite; a program needn't handle non-finite values.
Results may differ from a plain program's by a relative error of at most 0.0049.
Values may be sent and summed in bfloat16 or wider, within the bound.
A program may use at most 32 MiB of HBM per device.

v0:
```python
import jax
import jax.numpy as jnp
from jax import lax
from jax.sharding import PartitionSpec as P


def local(hidden, down_weight, expert_ids, combine, out_grad):
    dp_count = lax.axis_size("dp")
    tok_rows = expert_ids.shape[0]
    capacity = 2 * tok_rows // dp_count
    slot_count = dp_count * capacity
    feat_share = out_grad.shape[1]
    width = down_weight.shape[2]
    flat_ids = expert_ids.reshape(-1)
    labels = jnp.arange(dp_count, dtype=jnp.int32)
    onehot = (flat_ids[:, None] == labels[None, :]).astype(jnp.int32)
    pair_rank = jnp.sum((jnp.cumsum(onehot, axis=0) - 1) * onehot, axis=1)
    inside = flat_ids < dp_count
    target = jnp.where(inside, flat_ids * capacity + pair_rank, dp_count * capacity)
    weights = combine.reshape(-1)
    full_grad = lax.all_gather(out_grad, "cuts", axis=1, tiled=True)
    scaled = (weights[:, None] * jnp.repeat(full_grad, 2, axis=0).astype(jnp.float32)).astype(
        jnp.bfloat16
    )
    outgoing = (
        jnp.zeros((dp_count * capacity, width), jnp.bfloat16).at[target].set(scaled, mode="drop")
    )
    incoming = lax.all_to_all(
        outgoing.reshape(dp_count, capacity, width), "dp", split_axis=0, concat_axis=0, tiled=True
    )
    grad_rows = incoming.reshape(slot_count, width)
    hidden_rows = hidden[0]
    weight = down_weight[0]
    own_share = lax.psum_scatter(
        lax.dot_general(
            weight, hidden_rows, (((0,), (1,)), ((), ())), preferred_element_type=jnp.float32
        ),
        "cuts",
        scatter_dimension=0,
        tiled=True,
    )
    hid_grad = lax.dot_general(
        grad_rows, weight, (((1,), (1,)), ((), ())), preferred_element_type=jnp.float32
    ).astype(jnp.bfloat16)
    down_grad = lax.dot_general(
        hidden_rows, grad_rows, (((0,), (0,)), ((), ())), preferred_element_type=jnp.float32
    ).astype(jnp.bfloat16)
    returned = lax.all_to_all(
        own_share.astype(jnp.bfloat16), "dp", split_axis=1, concat_axis=1, tiled=True
    )
    pick_index = jnp.minimum(target, dp_count * capacity - 1)
    picked = jnp.take(returned, pick_index, axis=1).astype(jnp.float32)
    pair_coef = jnp.where(inside, weights, jnp.zeros_like(weights))
    summed = jnp.sum((picked * pair_coef[None, :]).reshape(feat_share, tok_rows, 2), axis=2)
    mixed = summed.T.astype(jnp.bfloat16)
    return (mixed, hid_grad[None], down_grad[None])


def solution(mesh):
    return jax.shard_map(
        local,
        mesh=mesh,
        in_specs=(
            P("dp", None, "cuts"),
            P("dp", "cuts", None),
            P("dp", None),
            P("dp", None),
            P("dp", "cuts"),
        ),
        out_specs=(P("dp", "cuts"), P("dp", None, "cuts"), P("dp", "cuts", None)),
        check_vma=False,
    )
```

profile of v0, /device:TPU:1, one launch (start us, length us, event | category | flops | bytes accessed | tf_op | source)
XLA Modules:
  0.0 511.5 jit_solution(12119890315271543798)
XLA Ops:
  7.2 0.0 copy-start
  7.2 0.9 copy.34
  8.1 0.1 eq.26
  8.2 0.1 reshape.132
  8.4 0.7 broadcast_multiply_fusion
  9.1 0.7 broadcast_select_fusion.1
  9.8 0.8 copy.43
  10.5 0.6 reduce-window.6
  11.1 0.2 slice_reduce_fusion
  11.4 0.1 copy.40
  11.5 0.2 lt.64
  11.7 0.1 copy.41
  11.8 0.1 mul.48
  11.9 124.1 %all_gather.3 = bf16[128,3072]{0,1:T(8,128)(2,1)} all-gather(bf16[128,96]{0,1:T(8,128)(2,1)} %param.9), channel_id=1, replica_groups=mesh['dp'=32,'cuts'=32] {'cuts'}, dimensions={1}, use_global_device_ids=true | all-gather | bytes 811008 | tf_op jit(solution)/shard_map/all_gather | solution.py:21
  136.0 1.4 copy.44
  137.4 0.0 copy-done.3
  137.4 2.7 broadcast_in_dim.40
  140.2 0.0 slice-start
  140.2 5.3 %convert_element_type.43 = f32[256,3072]{1,0:T(8,128)} reshape(f32[128,2,3072]{2,1,0:T(2,128)} %broadcast_in_dim.40) | data formatting | bytes 6291456 | tf_op jit(solution)/shard_map/convert_element_type | solution.py:22
  145.4 0.1 mul.51
  145.6 0.0 slice-done
  145.6 0.1 fusion.23
  145.7 5.4 %scatter_custom_fusion = bf16[256,3072]{1,0:T(8,128)(2,1)} fusion(s32[256]{0:T(256)S(1)} %bitcast.62, f32[256,3072]{1,0:T(8,128)} %convert_element_type.43, f32[256]{0:T(256)S(1)} %mul.51, bf16[]{:T(256)} %constant.36.clone.1), kind=kCustom, calls=%fused_computation.5 | custom fusion | flops 1572864 | bytes 4719618 | tf_op jit(solution)/shard_map/scatter | solution.py:26
  151.1 0.0 copy-start.1
  151.1 68.7 %all-to-all-start.1 = ((bf16[32,8,3072]{2,1,0:T(8,128)(2,1)}), bf16[32,8,3072]{2,1,0:T(8,128)(2,1)S(1)}, u32[]{:S(2)}, u32[]{:S(2)}) async-start(bf16[32,8,3072]{2,1,0:T(8,128)(2,1)} %bitcast.56), calls=%async_computation.2 | async-start | bytes 3145728 | tf_op jit(solution)/shard_map/all_to_all | solution.py:28
  219.8 0.0 reduce-scatter.2.cloned.1.call-start
  219.9 0.0 copy-done
  219.9 0.0 copy-done.1
  219.9 2.3 fusion.6
  222.2 0.0 copy-start.2
  222.2 0.0 reduce-scatter.2.cloned.1.call-update
  222.2 0.1 reduce_sum.23
  222.3 0.1 copy.37
  222.4 0.5 copy-done.2
  222.9 0.1 copy.38
  223.0 0.1 copy.42
  223.1 39.3 %all-to-all-done.1 = bf16[32,8,3072]{2,1,0:T(8,128)(2,1)S(1)} async-done(((bf16[32,8,3072]{2,1,0:T(8,128)(2,1)}), bf16[32,8,3072]{2,1,0:T(8,128)(2,1)S(1)}, u32[]{:S(2)}, u32[]{:S(2)}) %all-to-all-start.1) | async-done | bytes 1572896 | tf_op jit(solution)/shard_map/all_to_all | solution.py:28
  262.4 1.8 fusion
  264.2 2.6 copy.46
  266.8 180.6 %reduce-scatter.2.cloned.1.call-done = f32[96,256]{1,0:T(8,128)} async-done(((f32[3072,256]{1,0:T(8,128)}), f32[96,256]{1,0:T(8,128)}) %reduce-scatter.2.cloned.1.call-update) | async-done | bytes 98320 | tf_op jit(solution)/shard_map/reduce_scatter | solution.py:34
  447.3 0.9 convert_element_type.38
  448.2 0.7 copy.39
  449.0 36.9 %all-to-all-start = ((bf16[96,32,8]{0,2,1:T(8,128)(2,1)}), bf16[96,32,8]{0,2,1:T(8,128)(2,1)S(1)}, u32[]{:S(2)}, u32[]{:S(2)}) async-start(bf16[96,32,8]{0,2,1:T(8,128)(2,1)} %bitcast.3), calls=%async_computation.1 | async-start | bytes 131072 | tf_op jit(solution)/shard_map/all_to_all | solution.py:48
  485.8 1.3 fusion.14
  487.1 15.6 %all-to-all-done = bf16[96,32,8]{0,2,1:T(8,128)(2,1)S(1)} async-done(((bf16[96,32,8]{0,2,1:T(8,128)(2,1)}), bf16[96,32,8]{0,2,1:T(8,128)(2,1)S(1)}, u32[]{:S(2)}, u32[]{:S(2)}) %all-to-all-start) | async-done | bytes 49184 | tf_op jit(solution)/shard_map/all_to_all | solution.py:48
  502.7 0.9 gather_fusion
  503.6 0.4 multiply_reduce_fusion
  503.9 0.7 copy.45
  (6 shorter events, 0.1 us)
Async XLA Ops:
  7.2 212.7 %copy-start = (bf16[1,256,3072]{2,1,0:T(8,128)(2,1)S(1)}, bf16[1,256,3072]{2,1,0:T(8,128)(2,1)}, u32[]{:S(2)}) copy-start(bf16[1,256,3072]{2,1,0:T(8,128)(2,1)} %param.6) | copy-start | bytes 4718596
  11.4 126.0 %copy-start.3 = (s32[32,3]{0,1:T(4,128)}, s32[32,3]{0,1:T(4,128)S(1)}, u32[]{:S(2)}) copy-start(s32[32,3]{0,1:T(4,128)S(1)} %reduce-window.9) | copy-start | bytes 1156
  140.2 5.4 %slice-start = ((s32[32,3]{0,1:T(4,128)}), s32[32,2]{0,1:T(2,128)S(1)}, s32[]{:S(2)}) async-start(s32[32,3]{0,1:T(4,128)} %copy-done.3), calls=%async_computation.4 | async-start | bytes 2048 | tf_op jit(solution)/shard_map/slice.1
  151.1 68.7 %copy-start.1 = (bf16[1,256,256]{2,1,0:T(8,128)(2,1)S(1)}, bf16[1,256,256]{2,1,0:T(8,128)(2,1)}, u32[]{:S(2)}) copy-start(bf16[1,256,256]{2,1,0:T(8,128)(2,1)} %param.5) | copy-start | bytes 393220
  151.1 111.3 %all-to-all-start.1 = ((bf16[32,8,3072]{2,1,0:T(8,128)(2,1)}), bf16[32,8,3072]{2,1,0:T(8,128)(2,1)S(1)}, u32[]{:S(2)}, u32[]{:S(2)}) async-start(bf16[32,8,3072]{2,1,0:T(8,128)(2,1)} %bitcast.56), calls=%async_computation.2 | async-start | bytes 3145728 | tf_op jit(solution)/shard_map/all_to_all | solution.py:28
  219.8 227.5 %reduce-scatter.2.cloned.1.call-start = ((), (), s32[]{:S(2)}) async-start(), calls=%async_computation.3 | async-start | bytes 3244032 | tf_op jit(solution)/shard_map/reduce_scatter | solution.py:34
  222.2 0.7 copy-start.2
  449.0 53.8 %all-to-all-start = ((bf16[96,32,8]{0,2,1:T(8,128)(2,1)}), bf16[96,32,8]{0,2,1:T(8,128)(2,1)S(1)}, u32[]{:S(2)}, u32[]{:S(2)}) async-start(bf16[96,32,8]{0,2,1:T(8,128)(2,1)} %bitcast.3), calls=%async_computation.1 | async-start | bytes 131072 | tf_op jit(solution)/shard_map/all_to_all | solution.py:48
Sparse Core Ops, SparseCore 0:
  224.1 223.2 reduce-scatter.1
where the time goes:
time: 512 us; the launch traced here: 511 us
  waiting for transfers between devices  235 us (46%)
  blocking collectives  124 us (24%)
  starting transfers between devices  106 us (21%)
  local copies, waits for them, and re-layouts  18 us (4%)
  between operations  14.1 us (3%)
  other arithmetic  8.83 us (2%)
  matrix products  5.33 us (1%)
    reduce_scatter x1, waiting for transfers between devices, local(): lax.psum_scatter(lax.dot_general(weight, hidden_rows, (((0,), (1,)), ((),...  181 us
    all_gather x1, blocking collectives, local(): full_grad = lax.all_gather(out_grad, 'cuts', axis=1, tiled=True)  124 us
    all_to_all x1, starting transfers between devices, local(): lax.all_to_all(outgoing.reshape(dp_count, capacity, width), 'dp', split_a...  68.7 us
    all_to_all x1, waiting for transfers between devices, local(): lax.all_to_all(outgoing.reshape(dp_count, capacity, width), 'dp', split_a...  39.3 us
    all_to_all x1, starting transfers between devices, local(): lax.all_to_all(own_share.astype(jnp.bfloat16), 'dp', split_axis=1, concat...  36.9 us
    all_to_all x1, waiting for transfers between devices, local(): lax.all_to_all(own_share.astype(jnp.bfloat16), 'dp', split_axis=1, concat...  15.6 us
  transfers between devices with their start and end apart: 3, of which 3 were waited for; matrix products, arithmetic and copies ran while one was open for 2% of the time, Pallas kernels for 0%

commit v1 on v0

v1 whole, which is shorter than its diff:
```python
import functools

import jax
import jax.numpy as jnp
from jax import lax
from jax.experimental import pallas as pl
from jax.experimental.pallas import tpu as pltpu
from jax.sharding import PartitionSpec as P

MESH = pl.DeviceIdType.MESH
NX = 4
CAP = 8
BF = jnp.bfloat16
F32 = jnp.float32


def split_sum(onehot, rows):
    high = rows.astype(BF)
    low = (rows - high.astype(F32)).astype(BF)
    return jnp.dot(onehot, high, preferred_element_type=F32) + jnp.dot(
        onehot, low, preferred_element_type=F32
    )


def kernel(
    ndp,
    ncuts,
    hid_ref,
    weight_ref,
    term_ref,
    ids_ref,
    comb_ref,
    grad_ref,
    mixed_ref,
    hgrad_ref,
    wgrad_ref,
    out_buf,
    in_buf,
    gath,
    xrecv,
    xsum,
    zrecv,
    back_out,
    back_in,
    a_send,
    a_recv,
    c_send,
    c_recv,
    gz_send,
    gz_recv,
    gx_send,
    gx_recv,
    rx_send,
    rx_recv,
    rz_send,
    rz_recv,
):
    nz = ncuts // NX
    d = lax.axis_index("dp")
    c = lax.axis_index("cuts")
    z = c // NX
    x = lax.rem(c, NX)
    toks, share = grad_ref.shape
    slots = ndp * CAP

    def dp_peer(i):
        return lax.rem(d + i, ndp)

    def z_peer(i):
        return lax.rem(z + i, nz)

    def x_peer(i):
        return lax.rem(x + i, NX)

    barrier = pltpu.get_barrier_semaphore()

    def greet(i, carry):
        pl.semaphore_signal(barrier, inc=1, device_id={"dp": dp_peer(i)}, device_id_type=MESH)
        return carry

    lax.fori_loop(1, ndp, greet, 0)
    for i in range(1, nz):
        pl.semaphore_signal(
            barrier, inc=1, device_id={"cuts": z_peer(i) * NX + x}, device_id_type=MESH
        )
    for i in range(1, NX):
        pl.semaphore_signal(
            barrier, inc=1, device_id={"cuts": z * NX + x_peer(i)}, device_id_type=MESH
        )

    lane = lax.broadcasted_iota(jnp.int32, (toks, 128), 1)
    ids0 = ids_ref[:, 0:1]
    ids1 = ids_ref[:, 1:2]
    named0 = (lane == ids0) & (lane < ndp)
    named1 = (lane == ids1) & (lane < ndp)
    named = jnp.where(named0 | named1, 1.0, 0.0).astype(BF)
    row = lax.broadcasted_iota(jnp.int32, (toks, toks), 0)
    col = lax.broadcasted_iota(jnp.int32, (toks, toks), 1)
    before = jnp.where(col < row, 1.0, 0.0).astype(BF)
    count = jnp.dot(before, named, preferred_element_type=F32)
    rank0 = jnp.sum(jnp.where(named0, count, 0.0), axis=1, keepdims=True).astype(jnp.int32)
    rank1 = jnp.sum(jnp.where(named1, count, 0.0), axis=1, keepdims=True).astype(jnp.int32)
    place = lax.broadcasted_iota(jnp.int32, (toks, slots), 1)
    pick0 = jnp.where(place == ids0 * CAP + rank0, 1.0, 0.0)
    pick1 = jnp.where(place == ids1 * CAP + rank1, 1.0, 0.0)
    comb0 = comb_ref[:, 0:1]
    comb1 = comb_ref[:, 1:2]
    grad = grad_ref[...].astype(F32)
    scaled0 = (grad * comb0).astype(BF)
    scaled1 = (grad * comb1).astype(BF)
    rows = jnp.dot(pick0.T.astype(BF), scaled0, preferred_element_type=F32) + jnp.dot(
        pick1.T.astype(BF), scaled1, preferred_element_type=F32
    )
    out_buf[...] = jnp.zeros_like(out_buf)
    out_buf[:, :, :share] = rows.reshape(ndp, CAP, share)
    back_out[...] = jnp.zeros_like(back_out)

    pl.semaphore_wait(barrier, ndp - 1 + nz - 1 + NX - 1)

    def dp_copy(src, dst, send, recv, i):
        return pltpu.make_async_remote_copy(
            src_ref=src.at[dp_peer(i)],
            dst_ref=dst.at[d],
            send_sem=send.at[i],
            recv_sem=recv.at[d],
            device_id={"dp": dp_peer(i)},
            device_id_type=MESH,
        )

    def dp_arrival(src, dst, send, recv, i):
        return pltpu.make_async_remote_copy(
            src_ref=src.at[d],
            dst_ref=dst.at[dp_peer(i)],
            send_sem=send.at[i],
            recv_sem=recv.at[dp_peer(i)],
            device_id={"dp": dp_peer(i)},
            device_id_type=MESH,
        )

    def dp_start(src, dst, send, recv):
        def body(i, carry):
            dp_copy(src, dst, send, recv, i).start()
            return carry

        lax.fori_loop(1, ndp, body, 0)
        dst[d] = src[d]

    def dp_wait_recv(src, dst, send, recv):
        def body(i, carry):
            dp_arrival(src, dst, send, recv, i).wait_recv()
            return carry

        lax.fori_loop(1, ndp, body, 0)

    def dp_wait_send(src, dst, send, recv):
        def body(i, carry):
            dp_copy(src, dst, send, recv, i).wait_send()
            return carry

        lax.fori_loop(1, ndp, body, 0)

    def rx_copy(i, j):
        zz = z_peer(j)
        return pltpu.make_async_remote_copy(
            src_ref=term_ref.at[zz * NX + x_peer(i)],
            dst_ref=xrecv.at[i, j],
            send_sem=rx_send.at[i, j],
            recv_sem=rx_recv.at[i, j],
            device_id={"cuts": z * NX + x_peer(i)},
            device_id_type=MESH,
        )

    def rz_copy(j):
        return pltpu.make_async_remote_copy(
            src_ref=xsum.at[j],
            dst_ref=zrecv.at[j],
            send_sem=rz_send.at[j],
            recv_sem=rz_recv.at[j],
            device_id={"cuts": z_peer(j) * NX + x},
            device_id_type=MESH,
        )

    def gz_copy(j):
        return pltpu.make_async_remote_copy(
            src_ref=gath.at[c],
            dst_ref=gath.at[c],
            send_sem=gz_send.at[j],
            recv_sem=gz_recv.at[j],
            device_id={"cuts": z_peer(j) * NX + x},
            device_id_type=MESH,
        )

    def gz_arrival(j):
        block = lax.rem(z + nz - j, nz) * NX + x
        return pltpu.make_async_remote_copy(
            src_ref=gath.at[c],
            dst_ref=gath.at[block],
            send_sem=gz_send.at[j],
            recv_sem=gz_recv.at[j],
            device_id={"cuts": z_peer(j) * NX + x},
            device_id_type=MESH,
        )

    def gx_copy(i, j):
        block = lax.rem(z + nz - j, nz) * NX + x
        return pltpu.make_async_remote_copy(
            src_ref=gath.at[block],
            dst_ref=gath.at[block],
            send_sem=gx_send.at[i, j],
            recv_sem=gx_recv.at[i, j],
            device_id={"cuts": z * NX + x_peer(i)},
            device_id_type=MESH,
        )

    def gx_arrival(i, j):
        block = lax.rem(z + nz - j, nz) * NX + lax.rem(x + NX - i, NX)
        return pltpu.make_async_remote_copy(
            src_ref=gath.at[block],
            dst_ref=gath.at[block],
            send_sem=gx_send.at[i, j],
            recv_sem=gx_recv.at[i, j],
            device_id={"cuts": z * NX + x_peer(i)},
            device_id_type=MESH,
        )

    dp_start(out_buf, in_buf, a_send, a_recv)
    z_order = ZORDER(nz)
    for j in z_order + [0]:
        for i in (2, 1, 3):
            rx_copy(i, j).start()

    dp_wait_recv(out_buf, in_buf, a_send, a_recv)
    arrived = in_buf[...].reshape(slots, 128).T
    gath[c] = arrived[:share].astype(BF)
    for j in z_order:
        gz_copy(j).start()
    for i in (2, 1, 3):
        gx_copy(i, 0).start()

    for j in z_order:
        for i in range(1, NX):
            rx_copy(i, j).wait_recv()
        total = term_ref[z_peer(j) * NX + x].astype(F32)
        for i in range(1, NX):
            total = total + xrecv[i, j].astype(F32)
        xsum[j] = total.astype(BF)
        rz_copy(j).start()
    for i in range(1, NX):
        rx_copy(i, 0).wait_recv()
    own = term_ref[c].astype(F32)
    for i in range(1, NX):
        own = own + xrecv[i, 0].astype(F32)

    for j in z_order[::-1]:
        gz_arrival(j).wait_recv()
        for i in (2, 1, 3):
            gx_copy(i, j).start()

    for j in range(1, nz):
        rz_copy(j).wait_recv()
        own = own + zrecv[j].astype(F32)
    back_out[:, :, :share] = own.T.reshape(ndp, CAP, share)
    dp_start(back_out, back_in, c_send, c_recv)

    for j in range(nz):
        for i in range(1, NX):
            gx_arrival(i, j).wait_recv()
    width = ncuts * share
    full = gath[...].reshape(width, slots)
    hgrad_ref[...] = (
        jnp.dot(weight_ref[...], full, preferred_element_type=F32).T.astype(BF)
    )
    hid_t = hid_ref[...].astype(F32).T.astype(BF)
    step = width // 4
    for k in range(4):
        wgrad_ref[:, k * step : (k + 1) * step] = lax.dot_general(
            hid_t,
            full[k * step : (k + 1) * step],
            (((1,), (1,)), ((), ())),
            preferred_element_type=F32,
        ).astype(BF)

    dp_wait_recv(back_out, back_in, c_send, c_recv)
    expert_rows = back_in[...].reshape(slots, 128)
    mixed = comb0 * split_sum(pick0.astype(BF), expert_rows) + comb1 * split_sum(
        pick1.astype(BF), expert_rows
    )
    mixed_ref[...] = mixed[:, :share].astype(BF)

    dp_wait_send(out_buf, in_buf, a_send, a_recv)
    dp_wait_send(back_out, back_in, c_send, c_recv)
    for j in range(nz):
        if j:
            gz_copy(j).wait_send()
            rz_copy(j).wait_send()
        for i in range(1, NX):
            gx_copy(i, j).wait_send()
            rx_copy(i, j).wait_send()


def ZORDER(nz):
    return sorted(range(1, nz), key=lambda j: -min(j, nz - j))


def local(hidden, down_weight, expert_ids, combine, out_grad):
    ndp = lax.axis_size("dp")
    ncuts = lax.axis_size("cuts")
    nz = ncuts // NX
    toks, share = out_grad.shape
    hid = hidden[0]
    weight = down_weight[0]
    slots, ff = hid.shape
    width = weight.shape[1]
    terms = lax.dot_general(
        weight, hid, (((0,), (1,)), ((), ())), preferred_element_type=F32
    ).astype(BF)
    vm = pl.BlockSpec(memory_space=pltpu.VMEM)
    dma = pltpu.SemaphoreType.DMA
    mixed, hgrad, wgrad = pl.pallas_call(
        functools.partial(kernel, ndp, ncuts),
        out_shape=(
            jax.ShapeDtypeStruct((toks, share), BF),
            jax.ShapeDtypeStruct((slots, ff), BF),
            jax.ShapeDtypeStruct((ff, width), BF),
        ),
        in_specs=[vm] * 6,
        out_specs=(vm, vm, vm),
        scratch_shapes=[
            pltpu.VMEM((ndp, CAP, 128), F32),
            pltpu.VMEM((ndp, CAP, 128), F32),
            pltpu.VMEM((ncuts, share, slots), BF),
            pltpu.VMEM((NX, nz, share, slots), BF),
            pltpu.VMEM((nz, share, slots), BF),
            pltpu.VMEM((nz, share, slots), BF),
            pltpu.VMEM((ndp, CAP, 128), F32),
            pltpu.VMEM((ndp, CAP, 128), F32),
            dma((ndp,)),
            dma((ndp,)),
            dma((ndp,)),
            dma((ndp,)),
            dma((nz,)),
            dma((nz,)),
            dma((NX, nz)),
            dma((NX, nz)),
            dma((NX, nz)),
            dma((NX, nz)),
            dma((nz,)),
            dma((nz,)),
        ],
        compiler_params=pltpu.CompilerParams(collective_id=0, has_side_effects=True),
    )(hid, weight, terms.reshape(ncuts, share, slots), expert_ids, combine, out_grad)
    return (mixed, hgrad[None], wgrad[None])


def solution(mesh):
    return jax.shard_map(
        local,
        mesh=mesh,
        in_specs=(
            P("dp", None, "cuts"),
            P("dp", "cuts", None),
            P("dp", None),
            P("dp", None),
            P("dp", "cuts"),
        ),
        out_specs=(P("dp", "cuts"), P("dp", None, "cuts"), P("dp", "cuts", None)),
        check_vma=False,
    )
```

time: 512 us -> 102 us (0.20)
  the two profiles are of different devices: /device:TPU:1 before, /device:TPU:199 now
where the time goes in v1:
time: 102 us
  Pallas kernels  87.8 us (86%)
  local copies, waits for them, and re-layouts  9.95 us (10%)
  matrix products  3.18 us (3%)
    pallas_call x1, Pallas kernels, local(): pl.pallas_call(functools.partial(kernel, ndp, ncuts), out_shape=(jax.Shap...  87.8 us
    unnamed x6, local copies, waits for them, and re-layouts  9.95 us
    dot_general x1, matrix products, local(): lax.dot_general(weight, hid, (((0,), (1,)), ((), ())), preferred_element_...  3.18 us

profile of v1, /device:TPU:199, one launch (start us, length us, event | category | flops | bytes accessed | tf_op | source)
XLA Modules:
  0.0 101.5 jit_solution(12322339260539354908)
XLA Ops:
  0.6 1.5 %copy.10.grad_ref = bf16[128,96]{1,0:T(8,128)(2,1)} copy(bf16[128,96]{0,1:T(8,128)(2,1)} %param.9) | data formatting | bytes 49152 | tf_op args[4]
  2.1 1.4 %copy.8.ids_ref = s32[128,2]{1,0:T(8,128)} copy(s32[128,2]{0,1:T(2,128)} %param.7) | data formatting | bytes 2048 | tf_op args[2]
  3.5 1.4 %copy.9.comb_ref = f32[128,2]{1,0:T(8,128)} copy(f32[128,2]{0,1:T(2,128)} %param.8) | data formatting | bytes 2048 | tf_op args[3]
  4.9 3.2 %convolution_convert_fusion = bf16[3072,256]{1,0:T(8,128)(2,1)} fusion(bf16[1,256,3072]{2,1,0:T(8,128)(2,1)} %param.6, bf16[1,256,256]{2,1,0:T(8,128)(2,1)} %param.5), kind=kOutput, calls=%fused_computation | convolution fusion | flops 403439616 | bytes 3276800 | tf_op jit(solution)/shard_map/dot_general | solution.py:314
  8.1 87.8 %shard_map.76 = (bf16[128,96]{1,0:T(8,128)(2,1)}, bf16[256,256]{1,0:T(8,128)(2,1)}, bf16[256,3072]{1,0:T(8,128)(2,1)}) custom-call(bf16[256,256]{1,0:T(8,128)(2,1)} %bitcast.12, bf16[256,3072]{1,0:T(8,128)(2,1)} %bitcast.9, bf16[32,96,256]{2,1,0:T(8,128)(2,1)} %bitcast.10, s32[128,2]{1,0:T(8,128)} %copy.8.ids_ref, f32[128,2]{1,0:T(8,128)} %copy.9.comb_ref, ...), custom_call_target="tpu_custom_call" | custom-call | tf_op jit(solution)/shard_map/pallas_call | solution.py:319
  95.8 1.5 %copy.11 = bf16[128,96]{0,1:T(8,128)(2,1)} copy(bf16[128,96]{1,0:T(8,128)(2,1)} %get-tuple-element.9) | data formatting | bytes 49152
  97.3 1.6 %copy.14 = bf16[1,256,256]{2,1,0:T(8,128)(2,1)} copy(bf16[1,256,256]{2,1,0:T(8,128)(2,1)} %bitcast.13) | data formatting | bytes 262144
  98.9 2.7 %copy.15 = bf16[1,256,3072]{2,1,0:T(8,128)(2,1)} copy(bf16[1,256,3072]{2,1,0:T(8,128)(2,1)} %bitcast.11) | data formatting | bytes 3145728

commit v2 on v0

v2 whole, which is shorter than its diff:
```python
import functools

import jax
import jax.numpy as jnp
from jax import lax
from jax.experimental import pallas as pl
from jax.experimental.pallas import tpu as pltpu
from jax.sharding import PartitionSpec as P

MESH = pl.DeviceIdType.MESH
NX = 4
CAP = 8
BF = jnp.bfloat16
F32 = jnp.float32


def kernel(
    ndp,
    ncuts,
    hid_ref,
    weight_ref,
    term_ref,
    ids_ref,
    comb_ref,
    grad_ref,
    mixed_ref,
    hgrad_ref,
    wgrad_ref,
    out_buf,
    in_buf,
    back_out,
    back_in,
    gath,
    xrelay,
    xpair,
    xnear,
    xfar,
    xsum,
    zhalf,
    zout,
    zin,
    kept,
    a_send,
    a_recv,
    c_send,
    c_recv,
    x_send,
    x_recv,
    h_send,
    h_recv,
    m_send,
    m_recv,
    g_send,
    g_recv,
    gx_send,
    gx_recv,
):
    nz = ncuts // NX
    half = nz // 2
    d = lax.axis_index("dp")
    c = lax.axis_index("cuts")
    z = c // NX
    x = lax.rem(c, NX)
    h = z // half
    k = lax.rem(z, half)
    share, toks = grad_ref.shape
    slots = ndp * CAP

    order = [(o, m) for m in range(1, half) for o in (1, 0)] + [(1, 0), (0, 0)]

    def at(o, m):
        return o * half + m

    def z_block(o, m):
        side = h + o * (1 - 2 * h)
        return side * half + lax.rem(k + m + half, half)

    def cut(zz, xx):
        return zz * NX + lax.rem(xx + NX, NX)

    def dp_peer(i):
        return lax.rem(d + i, ndp)

    barrier = pltpu.get_barrier_semaphore()

    def greet(i, carry):
        pl.semaphore_signal(barrier, inc=1, device_id={"dp": dp_peer(i)}, device_id_type=MESH)
        return carry

    lax.fori_loop(1, ndp, greet, 0)
    near = [cut(z, x + 1), cut(z, x - 1), cut(z_block(1, 0), x)]
    near += [cut(z_block(0, m), x) for m in range(1, half)]
    for peer in near:
        pl.semaphore_signal(barrier, inc=1, device_id={"cuts": peer}, device_id_type=MESH)

    ids0 = ids_ref[0:1, :]
    ids1 = ids_ref[1:2, :]
    label = lax.broadcasted_iota(jnp.int32, (ndp, toks), 0)
    named0 = label == ids0
    named1 = label == ids1
    named = jnp.where(named0 | named1, 1.0, 0.0).astype(BF)
    row = lax.broadcasted_iota(jnp.int32, (toks, toks), 0)
    col = lax.broadcasted_iota(jnp.int32, (toks, toks), 1)
    before = jnp.where(row < col, 1.0, 0.0).astype(BF)
    count = jnp.dot(named, before, preferred_element_type=F32)
    rank0 = jnp.sum(jnp.where(named0, count, 0.0), axis=0, keepdims=True).astype(jnp.int32)
    rank1 = jnp.sum(jnp.where(named1, count, 0.0), axis=0, keepdims=True).astype(jnp.int32)
    place = lax.broadcasted_iota(jnp.int32, (slots, toks), 0)
    pick0 = jnp.where(place == ids0 * CAP + rank0, 1.0, 0.0).astype(BF)
    pick1 = jnp.where(place == ids1 * CAP + rank1, 1.0, 0.0).astype(BF)
    comb0 = comb_ref[0:1, :]
    comb1 = comb_ref[1:2, :]
    grad = grad_ref[...].astype(F32)
    rest = jnp.zeros((128 - share, toks), F32)
    scaled0 = jnp.concatenate([grad * comb0, rest], axis=0).astype(BF)
    scaled1 = jnp.concatenate([grad * comb1, rest], axis=0).astype(BF)
    last = (((1,), (1,)), ((), ()))
    rows = lax.dot_general(pick0, scaled0, last, preferred_element_type=F32) + lax.dot_general(
        pick1, scaled1, last, preferred_element_type=F32
    )
    out_buf[...] = rows.reshape(ndp, CAP, 128).astype(BF)

    pl.semaphore_wait(barrier, ndp - 1 + len(near))

    def dp_copy(src, dst, send, recv, i):
        return pltpu.make_async_remote_copy(
            src_ref=src.at[dp_peer(i)],
            dst_ref=dst.at[d],
            send_sem=send.at[i],
            recv_sem=recv.at[d],
            device_id={"dp": dp_peer(i)},
            device_id_type=MESH,
        )

    def dp_arrival(src, dst, send, recv, i):
        return pltpu.make_async_remote_copy(
            src_ref=src.at[d],
            dst_ref=dst.at[dp_peer(i)],
            send_sem=send.at[i],
            recv_sem=recv.at[dp_peer(i)],
            device_id={"dp": dp_peer(i)},
            device_id_type=MESH,
        )

    def dp_start(src, dst, send, recv):
        def body(i, carry):
            dp_copy(src, dst, send, recv, lax.rem(i + ndp // 2, ndp)).start()
            return carry

        lax.fori_loop(0, ndp // 2, body, 0)
        lax.fori_loop(ndp // 2 + 1, ndp, body, 0)
        dst[d] = src[d]

    def dp_wait_recv(src, dst, send, recv):
        def body(i, carry):
            dp_arrival(src, dst, send, recv, i).wait_recv()
            return carry

        lax.fori_loop(1, ndp, body, 0)

    def dp_wait_send(src, dst, send, recv):
        def body(i, carry):
            dp_copy(src, dst, send, recv, i).wait_send()
            return carry

        lax.fori_loop(1, ndp, body, 0)

    def cuts_copy(src, dst, send, recv, peer):
        return pltpu.make_async_remote_copy(
            src_ref=src,
            dst_ref=dst,
            send_sem=send,
            recv_sem=recv,
            device_id={"cuts": peer},
            device_id_type=MESH,
        )

    def way(o, m):
        return 1 if (o + m) % 2 == 0 else -1

    def rx_far(o, m):
        i, w = at(o, m), way(o, m)
        return cuts_copy(
            term_ref.at[cut(z_block(o, m), x + 2 * w)],
            xrelay.at[i],
            x_send.at[0, i],
            x_recv.at[0, i],
            cut(z, x + w),
        )

    def rx_pair(o, m):
        i, w = at(o, m), way(o, m)
        return cuts_copy(
            xpair.at[i], xfar.at[i], x_send.at[1, i], x_recv.at[1, i], cut(z, x + w)
        )

    def rx_near(o, m):
        i, w = at(o, m), way(o, m)
        return cuts_copy(
            term_ref.at[cut(z_block(o, m), x - w)],
            xnear.at[i],
            x_send.at[2, i],
            x_recv.at[2, i],
            cut(z, x - w),
        )

    def rh_copy(o, m):
        i = at(o, m)
        return cuts_copy(
            xsum.at[i], zhalf.at[i], h_send.at[i], h_recv.at[i], cut(z_block(0, m), x)
        )

    def rm_copy():
        return cuts_copy(zout, zin, m_send.at[0], m_recv.at[0], cut(z_block(1, 0), x))

    def g_own(m):
        return cuts_copy(
            gath.at[c], gath.at[c], g_send.at[m], g_recv.at[m], cut(z_block(0, m), x)
        )

    def g_mirror():
        return cuts_copy(
            gath.at[c],
            gath.at[c],
            g_send.at[half],
            g_recv.at[half],
            cut(z_block(1, 0), x),
        )

    def g_pass(m):
        block = cut(z_block(1, 0), x)
        return cuts_copy(
            gath.at[block],
            gath.at[block],
            g_send.at[half + m],
            g_recv.at[half + m],
            cut(z_block(0, m), x),
        )

    def g_arrival(o, m):
        block = cut(z_block(o, -m), x)
        return cuts_copy(
            gath.at[block],
            gath.at[block],
            g_send.at[at(o, m)],
            g_recv.at[at(o, m)],
            cut(z_block(0, m), x),
        )

    def gx_copy(o, m, w):
        i = at(o, m)
        s = 0 if w == 1 else 1
        block = cut(z_block(o, -m), x)
        return cuts_copy(
            gath.at[block],
            gath.at[block],
            gx_send.at[s, i],
            gx_recv.at[s, i],
            cut(z, x + w),
        )

    def gx_arrival(o, m, w):
        i = at(o, m)
        s = 0 if w == 1 else 1
        block = cut(z_block(o, -m), x - w)
        return cuts_copy(
            gath.at[block],
            gath.at[block],
            gx_send.at[s, i],
            gx_recv.at[s, i],
            cut(z, x + w),
        )

    def gx_relay(o, m):
        i, w = at(o, m), way(o, m)
        block = cut(z_block(o, -m), x - w)
        return cuts_copy(
            gath.at[block],
            gath.at[block],
            gx_send.at[2, i],
            gx_recv.at[2, i],
            cut(z, x + w),
        )

    def gx_relayed(o, m):
        i, w = at(o, m), way(o, m)
        block = cut(z_block(o, -m), x + 2)
        return cuts_copy(
            gath.at[block],
            gath.at[block],
            gx_send.at[2, i],
            gx_recv.at[2, i],
            cut(z, x + w),
        )

    dp_start(out_buf, in_buf, a_send, a_recv)
    for o, m in order:
        rx_far(o, m).start()
        rx_near(o, m).start()

    def relay_pair(o, m):
        i = at(o, m)
        rx_far(o, m).wait_recv()
        own = term_ref[cut(z_block(o, m), x + way(o, m))].astype(F32)
        xpair[i] = (xrelay[i].astype(F32) + own).astype(BF)
        rx_pair(o, m).start()

    def finish_x(o, m):
        i = at(o, m)
        rx_pair(o, m).wait_recv()
        rx_near(o, m).wait_recv()
        total = term_ref[cut(z_block(o, m), x)].astype(F32)
        total = total + xfar[i].astype(F32) + xnear[i].astype(F32)
        if m:
            xsum[i] = total.astype(BF)
            rh_copy(o, m).start()
        else:
            kept[o] = total

    lag = 2
    for n in range(len(order) + lag):
        if n < len(order):
            relay_pair(*order[n])
        if n >= lag:
            finish_x(*order[n - lag])

    dp_wait_recv(out_buf, in_buf, a_send, a_recv)
    arrived = in_buf[...].astype(F32).reshape(slots, 128).T
    gath[c] = arrived[:share].astype(BF)
    g_mirror().start()
    for m in range(1, half):
        g_own(m).start()
    gx_copy(0, 0, 1).start()
    gx_copy(0, 0, -1).start()

    across = kept[1]
    for m in range(1, half):
        rh_copy(1, m).wait_recv()
        across = across + zhalf[at(1, m)].astype(F32)
    zout[...] = across.astype(BF)
    rm_copy().start()
    own = kept[0]
    for m in range(1, half):
        rh_copy(0, m).wait_recv()
        own = own + zhalf[at(0, m)].astype(F32)
    rm_copy().wait_recv()
    own = own + zin[...].astype(F32)
    own = jnp.concatenate([own, jnp.zeros((128 - share, slots), F32)], axis=0)
    back_out[...] = own.T.reshape(ndp, CAP, 128).astype(BF)
    dp_start(back_out, back_in, c_send, c_recv)

    g_arrival(1, 0).wait_recv()
    for m in range(1, half):
        g_pass(m).start()
    gx_copy(1, 0, 1).start()
    gx_copy(1, 0, -1).start()

    turn = [(0, 0), (1, 0)] + [(0, m) for m in range(1, half)] + [(1, m) for m in range(1, half)]
    for n in range(len(turn) + lag):
        if 2 <= n < len(turn):
            o, m = turn[n]
            g_arrival(o, m).wait_recv()
            gx_copy(o, m, 1).start()
            gx_copy(o, m, -1).start()
        if n >= lag:
            o, m = turn[n - lag]
            gx_arrival(o, m, way(o, m)).wait_recv()
            gx_relay(o, m).start()
    for o, m in turn:
        gx_arrival(o, m, -way(o, m)).wait_recv()
        gx_relayed(o, m).wait_recv()

    width = ncuts * share
    full = gath[...].reshape(width, slots)
    hgrad_ref[...] = jnp.dot(weight_ref[...], full, preferred_element_type=F32).T.astype(BF)
    hid_t = hid_ref[...].astype(F32).T.astype(BF)
    step = width // 4
    for n in range(4):
        wgrad_ref[:, n * step : (n + 1) * step] = lax.dot_general(
            hid_t, full[n * step : (n + 1) * step], last, preferred_element_type=F32
        ).astype(BF)

    dp_wait_recv(back_out, back_in, c_send, c_recv)
    expert_rows = back_in[...].astype(F32).reshape(slots, 128).T[:share].astype(BF)
    mixed_ref[...] = (
        comb0 * jnp.dot(expert_rows, pick0, preferred_element_type=F32)
        + comb1 * jnp.dot(expert_rows, pick1, preferred_element_type=F32)
    ).astype(BF)

    dp_wait_send(out_buf, in_buf, a_send, a_recv)
    dp_wait_send(back_out, back_in, c_send, c_recv)
    rm_copy().wait_send()
    g_mirror().wait_send()
    for o, m in order:
        rx_far(o, m).wait_send()
        rx_near(o, m).wait_send()
        rx_pair(o, m).wait_send()
        gx_copy(o, m, 1).wait_send()
        gx_copy(o, m, -1).wait_send()
        gx_relay(o, m).wait_send()
        if m:
            rh_copy(o, m).wait_send()
            (g_pass(m) if o else g_own(m)).wait_send()


def local(hidden, down_weight, expert_ids, combine, out_grad):
    ndp = lax.axis_size("dp")
    ncuts = lax.axis_size("cuts")
    nz = ncuts // NX
    toks, share = out_grad.shape
    hid = hidden[0]
    weight = down_weight[0]
    slots, ff = hid.shape
    width = weight.shape[1]
    terms = lax.dot_general(
        weight, hid, (((0,), (1,)), ((), ())), preferred_element_type=F32
    ).astype(BF)
    vm = pl.BlockSpec(memory_space=pltpu.VMEM)
    dma = pltpu.SemaphoreType.DMA
    block = (share, slots)
    mixed, hgrad, wgrad = pl.pallas_call(
        functools.partial(kernel, ndp, ncuts),
        out_shape=(
            jax.ShapeDtypeStruct((share, toks), BF),
            jax.ShapeDtypeStruct((slots, ff), BF),
            jax.ShapeDtypeStruct((ff, width), BF),
        ),
        in_specs=[vm] * 6,
        out_specs=(vm, vm, vm),
        scratch_shapes=[pltpu.VMEM((ndp, CAP, 128), BF)] * 4
        + [pltpu.VMEM((ncuts,) + block, BF)]
        + [pltpu.VMEM((nz,) + block, BF)] * 6
        + [pltpu.VMEM(block, BF)] * 2
        + [pltpu.VMEM((2,) + block, F32)]
        + [dma((ndp,))] * 4
        + [dma((3, nz))] * 2
        + [dma((nz,))] * 2
        + [dma((1,))] * 2
        + [dma((nz,))] * 2
        + [dma((3, nz))] * 2,
        compiler_params=pltpu.CompilerParams(collective_id=0, has_side_effects=True),
    )(hid, weight, terms.reshape((ncuts,) + block), expert_ids.T, combine.T, out_grad.T)
    return (mixed.T, hgrad[None], wgrad[None])


def solution(mesh):
    return jax.shard_map(
        local,
        mesh=mesh,
        in_specs=(
            P("dp", None, "cuts"),
            P("dp", "cuts", None),
            P("dp", None),
            P("dp", None),
            P("dp", "cuts"),
        ),
        out_specs=(P("dp", "cuts"), P("dp", None, "cuts"), P("dp", "cuts", None)),
        check_vma=False,
    )
```

time: 512 us -> 94.9 us (0.19)
  the two profiles are of different devices: /device:TPU:1 before, /device:TPU:128 now
where the time goes in v2:
time: 94.9 us; the launch traced here: 94.6 us
  Pallas kernels  85.2 us (90%)
  local copies, waits for them, and re-layouts  5.56 us (6%)
  matrix products  3.18 us (3%)
    pallas_call x1, Pallas kernels, local(): pl.pallas_call(functools.partial(kernel, ndp, ncuts), out_shape=(jax.Shap...  85.2 us
    unnamed x3, local copies, waits for them, and re-layouts  5.56 us
    dot_general x1, matrix products, local(): lax.dot_general(weight, hid, (((0,), (1,)), ((), ())), preferred_element_...  3.18 us

profile of v2, /device:TPU:128, one launch (start us, length us, event | category | flops | bytes accessed | tf_op | source)
XLA Modules:
  0.0 94.6 jit_solution(34225826217047812)
XLA Ops:
  0.6 3.2 %convolution_convert_fusion = bf16[3072,256]{1,0:T(8,128)(2,1)} fusion(bf16[1,256,3072]{2,1,0:T(8,128)(2,1)} %param.6, bf16[1,256,256]{2,1,0:T(8,128)(2,1)} %param.5), kind=kOutput, calls=%fused_computation | convolution fusion | flops 403439616 | bytes 3276800 | tf_op jit(solution)/shard_map/dot_general | solution.py:415
  3.8 85.2 %shard_map.76 = (bf16[96,128]{1,0:T(8,128)(2,1)}, bf16[256,256]{1,0:T(8,128)(2,1)}, bf16[256,3072]{1,0:T(8,128)(2,1)}) custom-call(bf16[256,256]{1,0:T(8,128)(2,1)} %bitcast.16, bf16[256,3072]{1,0:T(8,128)(2,1)} %bitcast.13, bf16[32,96,256]{2,1,0:T(8,128)(2,1)} %bitcast.14, s32[2,128]{1,0:T(2,128)} %bitcast.20, f32[2,128]{1,0:T(2,128)} %bitcast.21, ...), custom_call_target="tpu_custom_call" | custom-call | tf_op jit(solution)/shard_map/pallas_call | solution.py:421
  89.0 1.3 %copy.11 = bf16[128,96]{0,1:T(8,128)(2,1)} copy(bf16[128,96]{0,1:T(8,128)(2,1)} %bitcast.19) | data formatting | bytes 49152
  90.4 1.6 %copy.12 = bf16[1,256,256]{2,1,0:T(8,128)(2,1)} copy(bf16[1,256,256]{2,1,0:T(8,128)(2,1)} %bitcast.17) | data formatting | bytes 262144
  91.9 2.7 %copy.13 = bf16[1,256,3072]{2,1,0:T(8,128)(2,1)} copy(bf16[1,256,3072]{2,1,0:T(8,128)(2,1)} %bitcast.15) | data formatting | bytes 3145728

commit v3 on v2

--- a/solution.py
+++ b/solution.py
@@ -27,8 +27,12 @@
     hgrad_ref,
     wgrad_ref,
     out_buf,
+    out_mid,
+    out_hop,
     in_buf,
     back_out,
+    back_mid,
+    back_hop,
     back_in,
     gath,
     xrelay,
@@ -78,16 +82,23 @@
     def cut(zz, xx):
         return zz * NX + lax.rem(xx + NX, NX)
 
-    def dp_peer(i):
-        return lax.rem(d + i, ndp)
+    ny = ndp // 4
+    y = d // 4
+    zh = lax.rem(d // 2, 2)
+    co = lax.rem(d, 2)
+
+    def dp_at(yy, zz, cc):
+        return (yy * 2 + zz) * 2 + cc
+
+    def y_peer(i):
+        return lax.rem(y + i + ny, ny)
 
     barrier = pltpu.get_barrier_semaphore()
 
-    def greet(i, carry):
-        pl.semaphore_signal(barrier, inc=1, device_id={"dp": dp_peer(i)}, device_id_type=MESH)
-        return carry
-
-    lax.fori_loop(1, ndp, greet, 0)
+    others = [dp_at(y, 1 - zh, co), dp_at(y, zh, 1 - co)]
+    others += [dp_at(y_peer(i), zh, co) for i in range(1, ny)]
+    for peer in others:
+        pl.semaphore_signal(barrier, inc=1, device_id={"dp": peer}, device_id_type=MESH)
     near = [cut(z, x + 1), cut(z, x - 1), cut(z_block(1, 0), x)]
     near += [cut(z_block(0, m), x) for m in range(1, half)]
     for peer in near:
@@ -118,52 +129,69 @@
     rows = lax.dot_general(pick0, scaled0, last, preferred_element_type=F32) + lax.dot_general(
         pick1, scaled1, last, preferred_element_type=F32
     )
-    out_buf[...] = rows.reshape(ndp, CAP, 128).astype(BF)
-
-    pl.semaphore_wait(barrier, ndp - 1 + len(near))
-
-    def dp_copy(src, dst, send, recv, i):
-        return pltpu.make_async_remote_copy(
-            src_ref=src.at[dp_peer(i)],
-            dst_ref=dst.at[d],
-            send_sem=send.at[i],
-            recv_sem=recv.at[d],
-            device_id={"dp": dp_peer(i)},
-            device_id_type=MESH,
-        )
-
-    def dp_arrival(src, dst, send, recv, i):
-        return pltpu.make_async_remote_copy(
-            src_ref=src.at[d],
-            dst_ref=dst.at[dp_peer(i)],
-            send_sem=send.at[i],
-            recv_sem=recv.at[dp_peer(i)],
-            device_id={"dp": dp_peer(i)},
-            device_id_type=MESH,
-        )
-
-    def dp_start(src, dst, send, recv):
-        def body(i, carry):
-            dp_copy(src, dst, send, recv, lax.rem(i + ndp // 2, ndp)).start()
-            return carry
-
-        lax.fori_loop(0, ndp // 2, body, 0)
-        lax.fori_loop(ndp // 2 + 1, ndp, body, 0)
-        dst[d] = src[d]
-
-    def dp_wait_recv(src, dst, send, recv):
-        def body(i, carry):
-            dp_arrival(src, dst, send, recv, i).wait_recv()
-            return carry
-
-        lax.fori_loop(1, ndp, body, 0)
-
-    def dp_wait_send(src, dst, send, recv):
-        def body(i, carry):
-            dp_copy(src, dst, send, recv, i).wait_send()
-            return carry
-
-        lax.fori_loop(1, ndp, body, 0)
+    out_buf[...] = rows.reshape(ny, 2, 2, CAP, 128).astype(BF)
+
+    pl.semaphore_wait(barrier, len(others) + len(near))
+
+    class Exchange:
+        def __init__(self, src, mid, hop, dst, send, recv):
+            self.src, self.mid, self.hop, self.dst = src, mid, hop, dst
+            self.send, self.recv = send, recv
+
+        def copy(self, src, dst, n, peer):
+            return pltpu.make_async_remote_copy(
+                src_ref=src,
+                dst_ref=dst,
+                send_sem=self.send.at[n],
+                recv_sem=self.recv.at[n],
+                device_id={"dp": peer},
+                device_id_type=MESH,
+            )
+
+        def step(self, n, arrival=False):
+            far, sibling = dp_at(y, 1 - zh, co), dp_at(y, zh, 1 - co)
+            src, mid, hop = self.src, self.mid, self.hop
+            if n == 0:
+                land = mid.at[:, 1 - zh, co] if arrival else mid.at[:, zh, co]
+                return self.copy(src.at[:, 1 - zh, co], land, 0, far)
+            if n == 1:
+                return self.copy(src.at[:, 1 - zh, 1 - co], hop, 1, far)
+            if n == 2:
+                land = mid.at[:, zh, 1 - co] if arrival else mid.at[:, zh, co]
+                return self.copy(src.at[:, zh, 1 - co], land, 2, sibling)
+            if n == 3:
+                land = mid.at[:, 1 - zh, 1 - co] if arrival else mid.at[:, 1 - zh, co]
+                return self.copy(hop, land, 3, sibling)
+            i = n - 3
+            land = self.dst.at[y_peer(-i)] if arrival else self.dst.at[y]
+            return self.copy(mid.at[y_peer(i)], land, n, dp_at(y_peer(i), zh, co))
+
+        def start(self):
+            for n in (1, 0, 2):
+                self.step(n).start()
+            self.mid[:, zh, co] = self.src[:, zh, co]
+
+        def cross(self):
+            self.step(1, True).wait_recv()
+            self.step(3).start()
+
+        def spread(self):
+            for n in (2, 0, 3):
+                self.step(n, True).wait_recv()
+            for i in sorted(range(1, ny), key=lambda i: -min(i, ny - i)):
+                self.step(3 + i).start()
+            self.dst[y] = self.mid[y]
+
+        def wait(self):
+            for i in range(1, ny):
+                self.step(3 + i, True).wait_recv()
+
+        def done(self):
+            for n in range(3 + ny):
+                self.step(n).wait_send()
+
+    there = Exchange(out_buf, out_mid, out_hop, in_buf, a_send, a_recv)
+    back = Exchange(back_out, back_mid, back_hop, back_in, c_send, c_recv)
 
     def cuts_copy(src, dst, send, recv, peer):
         return pltpu.make_async_remote_copy(
@@ -293,7 +321,7 @@
             cut(z, x + w),
         )
 
-    dp_start(out_buf, in_buf, a_send, a_recv)
+    there.start()
     for o, m in order:
         rx_far(o, m).start()
         rx_near(o, m).start()
@@ -319,12 +347,15 @@
 
     lag = 2
     for n in range(len(order) + lag):
+        if n == len(order) // 2:
+            there.cross()
+            there.spread()
         if n < len(order):
             relay_pair(*order[n])
         if n >= lag:
             finish_x(*order[n - lag])
 
-    dp_wait_recv(out_buf, in_buf, a_send, a_recv)
+    there.wait()
     arrived = in_buf[...].astype(F32).reshape(slots, 128).T
     gath[c] = arrived[:share].astype(BF)
     g_mirror().start()
@@ -346,8 +377,8 @@
     rm_copy().wait_recv()
     own = own + zin[...].astype(F32)
     own = jnp.concatenate([own, jnp.zeros((128 - share, slots), F32)], axis=0)
-    back_out[...] = own.T.reshape(ndp, CAP, 128).astype(BF)
-    dp_start(back_out, back_in, c_send, c_recv)
+    back_out[...] = own.T.reshape(ny, 2, 2, CAP, 128).astype(BF)
+    back.start()
 
     g_arrival(1, 0).wait_recv()
     for m in range(1, half):
@@ -357,6 +388,9 @@
 
     turn = [(0, 0), (1, 0)] + [(0, m) for m in range(1, half)] + [(1, m) for m in range(1, half)]
     for n in range(len(turn) + lag):
+        if n == len(turn) // 2 + 1:
+            back.cross()
+            back.spread()
         if 2 <= n < len(turn):
             o, m = turn[n]
             g_arrival(o, m).wait_recv()
@@ -380,15 +414,15 @@
             hid_t, full[n * step : (n + 1) * step], last, preferred_element_type=F32
         ).astype(BF)
 
-    dp_wait_recv(back_out, back_in, c_send, c_recv)
+    back.wait()
     expert_rows = back_in[...].astype(F32).reshape(slots, 128).T[:share].astype(BF)
     mixed_ref[...] = (
         comb0 * jnp.dot(expert_rows, pick0, preferred_element_type=F32)
         + comb1 * jnp.dot(expert_rows, pick1, preferred_element_type=F32)
     ).astype(BF)
 
-    dp_wait_send(out_buf, in_buf, a_send, a_recv)
-    dp_wait_send(back_out, back_in, c_send, c_recv)
+    there.done()
+    back.done()
     rm_copy().wait_send()
     g_mirror().wait_send()
     for o, m in order:
@@ -427,12 +461,18 @@
         ),
         in_specs=[vm] * 6,
         out_specs=(vm, vm, vm),
-        scratch_shapes=[pltpu.VMEM((ndp, CAP, 128), BF)] * 4
+        scratch_shapes=[
+            pltpu.VMEM((ndp // 4, 2, 2, CAP, 128), BF),
+            pltpu.VMEM((ndp // 4, 2, 2, CAP, 128), BF),
+            pltpu.VMEM((ndp // 4, CAP, 128), BF),
+            pltpu.VMEM((ndp // 4, 2, 2, CAP, 128), BF),
+        ]
+        * 2
         + [pltpu.VMEM((ncuts,) + block, BF)]
         + [pltpu.VMEM((nz,) + block, BF)] * 6
         + [pltpu.VMEM(block, BF)] * 2
         + [pltpu.VMEM((2,) + block, F32)]
-        + [dma((ndp,))] * 4
+        + [dma((ndp // 4 + 3,))] * 4
         + [dma((3, nz))] * 2
         + [dma((nz,))] * 2
         + [dma((1,))] * 2

time: 94.9 us -> 88 us (0.927)
  Pallas kernels: 85.2 us -> 78.3 us
    pallas_call x1, Pallas kernels: 85.2 us -> 78.3 us  [local(): pl.pallas_call(functools.partial(kernel, ndp, ncuts), out_shape=(jax.Shap...]
where the time goes in v3:
time: 88 us; the launch traced here: 87.7 us
  Pallas kernels  78.3 us (89%)
  local copies, waits for them, and re-layouts  5.56 us (6%)
  matrix products  3.18 us (4%)
    pallas_call x1, Pallas kernels, local(): pl.pallas_call(functools.partial(kernel, ndp, ncuts), out_shape=(jax.Shap...  78.3 us
    unnamed x3, local copies, waits for them, and re-layouts  5.56 us
    dot_general x1, matrix products, local(): lax.dot_general(weight, hid, (((0,), (1,)), ((), ())), preferred_element_...  3.18 us

profile of v3, /device:TPU:128, one launch (start us, length us, event | category | flops | bytes accessed | tf_op | source)
XLA Modules:
  0.0 87.7 jit_solution(4501826649980733500)
XLA Ops:
  0.6 3.2 %convolution_convert_fusion = bf16[3072,256]{1,0:T(8,128)(2,1)} fusion(bf16[1,256,3072]{2,1,0:T(8,128)(2,1)} %param.6, bf16[1,256,256]{2,1,0:T(8,128)(2,1)} %param.5), kind=kOutput, calls=%fused_computation | convolution fusion | flops 403439616 | bytes 3276800 | tf_op jit(solution)/shard_map/dot_general | solution.py:449
  3.8 78.3 %shard_map.76 = (bf16[96,128]{1,0:T(8,128)(2,1)}, bf16[256,256]{1,0:T(8,128)(2,1)}, bf16[256,3072]{1,0:T(8,128)(2,1)}) custom-call(bf16[256,256]{1,0:T(8,128)(2,1)} %bitcast.16, bf16[256,3072]{1,0:T(8,128)(2,1)} %bitcast.13, bf16[32,96,256]{2,1,0:T(8,128)(2,1)} %bitcast.14, s32[2,128]{1,0:T(2,128)} %bitcast.20, f32[2,128]{1,0:T(2,128)} %bitcast.21, ...), custom_call_target="tpu_custom_call" | custom-call | tf_op jit(solution)/shard_map/pallas_call | solution.py:455
  82.1 1.3 %copy.11 = bf16[128,96]{0,1:T(8,128)(2,1)} copy(bf16[128,96]{0,1:T(8,128)(2,1)} %bitcast.19) | data formatting | bytes 49152
  83.5 1.6 %copy.12 = bf16[1,256,256]{2,1,0:T(8,128)(2,1)} copy(bf16[1,256,256]{2,1,0:T(8,128)(2,1)} %bitcast.17) | data formatting | bytes 262144
  85.0 2.7 %copy.13 = bf16[1,256,3072]{2,1,0:T(8,128)(2,1)} copy(bf16[1,256,3072]{2,1,0:T(8,128)(2,1)} %bitcast.15) | data formatting | bytes 3145728

commit v4 on v3

--- a/solution.py
+++ b/solution.py
@@ -19,13 +19,13 @@
     ncuts,
     hid_ref,
     weight_ref,
-    term_ref,
     ids_ref,
     comb_ref,
     grad_ref,
     mixed_ref,
     hgrad_ref,
     wgrad_ref,
+    term_ref,
     out_buf,
     out_mid,
     out_hop,
@@ -131,6 +131,20 @@
     )
     out_buf[...] = rows.reshape(ny, 2, 2, CAP, 128).astype(BF)
 
+    hid_t = hid_ref[...].astype(F32).T.astype(BF)
+    width = ncuts * share
+    step = width // 4
+    for n in range(4):
+        term = lax.dot_general(
+            weight_ref[:, n * step : (n + 1) * step],
+            hid_t,
+            (((0,), (0,)), ((), ())),
+            preferred_element_type=F32,
+        )
+        term_ref[n * (ncuts // 4) : (n + 1) * (ncuts // 4)] = term.astype(BF).reshape(
+            ncuts // 4, share, slots
+        )
+
     pl.semaphore_wait(barrier, len(others) + len(near))
 
     class Exchange:
@@ -404,11 +418,8 @@
         gx_arrival(o, m, -way(o, m)).wait_recv()
         gx_relayed(o, m).wait_recv()
 
-    width = ncuts * share
     full = gath[...].reshape(width, slots)
     hgrad_ref[...] = jnp.dot(weight_ref[...], full, preferred_element_type=F32).T.astype(BF)
-    hid_t = hid_ref[...].astype(F32).T.astype(BF)
-    step = width // 4
     for n in range(4):
         wgrad_ref[:, n * step : (n + 1) * step] = lax.dot_general(
             hid_t, full[n * step : (n + 1) * step], last, preferred_element_type=F32
@@ -446,9 +457,6 @@
     weight = down_weight[0]
     slots, ff = hid.shape
     width = weight.shape[1]
-    terms = lax.dot_general(
-        weight, hid, (((0,), (1,)), ((), ())), preferred_element_type=F32
-    ).astype(BF)
     vm = pl.BlockSpec(memory_space=pltpu.VMEM)
     dma = pltpu.SemaphoreType.DMA
     block = (share, slots)
@@ -459,9 +467,10 @@
             jax.ShapeDtypeStruct((slots, ff), BF),
             jax.ShapeDtypeStruct((ff, width), BF),
         ),
-        in_specs=[vm] * 6,
+        in_specs=[vm] * 5,
         out_specs=(vm, vm, vm),
-        scratch_shapes=[
+        scratch_shapes=[pltpu.VMEM((ncuts,) + block, BF)]
+        + [
             pltpu.VMEM((ndp // 4, 2, 2, CAP, 128), BF),
             pltpu.VMEM((ndp // 4, 2, 2, CAP, 128), BF),
             pltpu.VMEM((ndp // 4, CAP, 128), BF),
@@ -479,7 +488,7 @@
         + [dma((nz,))] * 2
         + [dma((3, nz))] * 2,
         compiler_params=pltpu.CompilerParams(collective_id=0, has_side_effects=True),
-    )(hid, weight, terms.reshape((ncuts,) + block), expert_ids.T, combine.T, out_grad.T)
+    )(hid, weight, expert_ids.T, combine.T, out_grad.T)
     return (mixed.T, hgrad[None], wgrad[None])
 
 

time: 88 us -> 84.3 us (0.958)
  matrix products: 3.18 us -> 0 us
    dot_general x1 -> x0, matrix products: 3.18 us -> none  [local(): lax.dot_general(weight, hid, (((0,), (1,)), ((), ())), preferred_element_...]
where the time goes in v4:
time: 84.3 us; the launch traced here: 84 us
  Pallas kernels  77.8 us (92%)
  local copies, waits for them, and re-layouts  5.56 us (7%)
    pallas_call x1, Pallas kernels, local(): pl.pallas_call(functools.partial(kernel, ndp, ncuts), out_shape=(jax.Shap...  77.8 us
    unnamed x3, local copies, waits for them, and re-layouts  5.56 us

profile of v4, /device:TPU:128, one launch (start us, length us, event | category | flops | bytes accessed | tf_op | source)
XLA Modules:
  0.0 84.0 jit_solution(12177302820258451415)
XLA Ops:
  0.6 77.8 %shard_map.76 = (bf16[96,128]{1,0:T(8,128)(2,1)}, bf16[256,256]{1,0:T(8,128)(2,1)}, bf16[256,3072]{1,0:T(8,128)(2,1)}) custom-call(bf16[256,256]{1,0:T(8,128)(2,1)} %bitcast.11, bf16[256,3072]{1,0:T(8,128)(2,1)} %bitcast.9, s32[2,128]{1,0:T(2,128)} %bitcast.14, f32[2,128]{1,0:T(2,128)} %bitcast.15, bf16[96,128]{1,0:T(8,128)(2,1)} %bitcast.13), custom_call_target="tpu_custom_call" | custom-call | tf_op jit(solution)/shard_map/pallas_call | solution.py:463
  78.4 1.3 %copy.11 = bf16[128,96]{0,1:T(8,128)(2,1)} copy(bf16[128,96]{0,1:T(8,128)(2,1)} %bitcast.12) | data formatting | bytes 49152
  79.8 1.6 %copy.12 = bf16[1,256,256]{2,1,0:T(8,128)(2,1)} copy(bf16[1,256,256]{2,1,0:T(8,128)(2,1)} %bitcast.10) | data formatting | bytes 262144
  81.3 2.7 %copy.13 = bf16[1,256,3072]{2,1,0:T(8,128)(2,1)} copy(bf16[1,256,3072]{2,1,0:T(8,128)(2,1)} %bitcast.8) | data formatting | bytes 3145728
